TPU v7x, 128 devices: a whole 4x4x4 slice. The times are simulated.
128 devices in a mesh: img: 16 (over z, x), pen: 8 (over y, core).
Axes of the slice: x: 4, y: 4, z: 4, core: 2. Of those that a mesh axis runs over, the one named last changes fastest.
Arguments:
- slice_tiles: bfloat16 [8192, 128, 256], P(('img', 'pen')), may hold values from -192 to 192
- ctf_tiles: bfloat16 [8192, 128, 128], P(('img', 'pen')), may hold values from 0.25 to 16
- entry_tile: int32 [16384], P(('img', 'pen')), may hold values from 0 to 63
- entry_brick: int32 [16384, 1], P(('img', 'pen')), may hold values from 0 to 127; in each aligned block of 128 rows (0 to 127, 128 to 255, ...) at most 2 rows name the same one
- entry_kernel: int32 [16384], P(('img', 'pen')), may hold values from 0 to 15
- ky_bank: bfloat16 [16, 48, 128], replicated, may hold values from 0 to 1
- kx_bank: bfloat16 [16, 128, 384], replicated, may hold values from 0 to 1
- z_bank: bfloat16 [16, 128], replicated, may hold values from 0.099609375 to 1
Outputs:
- volume: float32 [768, 768, 128], P('pen', 'img')
Inputs may be any that keep to these rules, and one draw needn't show every extreme that they name: `entry_brick`: within the rows of one device no brick is named more than 2 times, a bound that some block reaches. `entry_tile`: an index among the 64 tiles of the entry's own device.
All inputs are finite; a program needn't handle non-finite values.
Results may differ from a plain program's by a relative error of at most 0.0041.
Values may be sent and summed in bfloat16 or wider, within the bound.
A program may use at most 192 MiB of HBM per device.

v0:
```python
import math

import jax
import jax.numpy as jnp
from jax import lax
from jax.sharding import PartitionSpec as P

NBOX = 768
KXH = 384
PIX = 128
NK = 16
CAP = 2
ZW = 128


def angle_table(left_idx, right_idx):
    product = left_idx[:, None] * right_idx[None, :] % NBOX
    return 2.0 * math.pi / NBOX * product.astype(jnp.float32)


def local(slice_tiles, ctf_tiles, entry_tile, entry_brick, entry_kernel, ky_bank, kx_bank, z_bank):
    img_count = lax.axis_size("img")
    pen_count = lax.axis_size("pen")
    bricks = img_count * pen_count
    entry_count = entry_tile.shape[0]
    rows_brick = ky_bank.shape[1]
    window = z_bank.shape[1]
    planes = window // pen_count
    slot_total = bricks * CAP
    images = jnp.concatenate([slice_tiles, ctf_tiles], axis=2)
    target = entry_brick[:, 0]
    positions = jnp.arange(entry_count, dtype=jnp.int32)
    earlier = (target[None, :] == target[:, None]) & (positions[None, :] < positions[:, None])
    slot_rank = jnp.sum(earlier.astype(jnp.int32), axis=1)
    slot_index = target * CAP + slot_rank
    pixels = images[entry_tile]
    half_tile = jnp.einsum(
        "eyp,epc->eyc", ky_bank[entry_kernel], pixels, preferred_element_type=jnp.float32
    ).astype(jnp.bfloat16)
    shaped = half_tile.reshape(half_tile.shape[0], rows_brick, 3, PIX)
    gridded = jnp.einsum(
        "sycp,spq->sycq", shaped, kx_bank[entry_kernel], preferred_element_type=jnp.float32
    )
    payload = gridded.astype(jnp.bfloat16).reshape(half_tile.shape[0], rows_brick, 3 * KXH)
    tile_width = payload.shape[2]
    outgoing = (
        jnp.zeros((slot_total, rows_brick, tile_width), jnp.bfloat16).at[slot_index].set(payload)
    )
    labels = jnp.zeros((slot_total,), jnp.int32).at[slot_index].set(entry_kernel)
    incoming, kind_ids = (
        lax.all_to_all(outgoing, ("img", "pen"), split_axis=0, concat_axis=0, tiled=True),
        lax.all_to_all(labels, ("img", "pen"), split_axis=0, concat_axis=0, tiled=True),
    )
    plane_start = lax.axis_index("pen") * planes
    z_columns = lax.dynamic_slice_in_dim(z_bank, plane_start, planes, 1)
    onehot = (kind_ids[:, None] == jnp.arange(NK, dtype=jnp.int32)[None, :]).astype(jnp.bfloat16)
    weights_z = jnp.dot(onehot, z_columns, preferred_element_type=jnp.float32).astype(jnp.bfloat16)
    brick_sums = jnp.dot(
        weights_z.T, incoming.reshape(slot_total, -1), preferred_element_type=jnp.float32
    ).reshape(planes, rows_brick, 3, KXH)
    denominator = brick_sums[:, :, 2] + 1.0
    grid_real = brick_sums[:, :, 0] / denominator
    grid_imag = brick_sums[:, :, 1] / denominator
    kx_idx = jnp.arange(KXH, dtype=jnp.int32)
    box_idx = jnp.arange(NBOX, dtype=jnp.int32)
    angles_x = angle_table(kx_idx, box_idx)
    weight_x = jnp.where(kx_idx == 0, 1.0, 2.0).astype(jnp.float32)[:, None]
    cos_x = weight_x * jnp.cos(angles_x)
    sin_x = weight_x * jnp.sin(angles_x)
    table_x = jnp.concatenate(
        [jnp.stack([cos_x, sin_x], -1), jnp.stack([-sin_x, cos_x], -1)], 0
    ).reshape(2 * KXH, 2 * NBOX)
    angles_y = angle_table(box_idx, box_idx)
    cos_y = jnp.cos(angles_y)
    sin_y = jnp.sin(angles_y)
    table_y = jnp.stack([jnp.stack([cos_y, sin_y], -1), jnp.stack([-sin_y, cos_y], -1)], 1)
    angles_z = angle_table(jnp.arange(window, dtype=jnp.int32), jnp.arange(ZW, dtype=jnp.int32))
    table_z = jnp.stack([jnp.cos(angles_z), -jnp.sin(angles_z)], 1)
    norm_scale = 1.0 / math.sqrt(window * NBOX * KXH)
    stacked = jnp.concatenate([grid_real, grid_imag], axis=2).reshape(planes * rows_brick, 2 * KXH)
    after_x = jnp.dot(stacked, table_x, precision=lax.Precision.HIGHEST).reshape(
        planes, rows_brick, 2 * NBOX
    )
    block_in = lax.all_to_all(after_x, "img", split_axis=2, concat_axis=1, tiled=True)
    items = block_in.shape[0]
    shaped = block_in.reshape(items, NBOX, -1, 2)
    result = jnp.einsum("nkxc,kcyd->nyxd", shaped, table_y, precision=lax.Precision.HIGHEST)
    after_y = result.reshape(items, NBOX, -1)
    return (
        jnp.einsum(
            "kyxc,kcz->yxz",
            lax.all_to_all(
                after_y.reshape(planes, NBOX, -1, 2), "pen", split_axis=1, concat_axis=0, tiled=True
            ),
            table_z,
            precision=lax.Precision.HIGHEST,
        )
        * norm_scale
    )


def solution(mesh):
    return jax.shard_map(
        local,
        mesh=mesh,
        in_specs=(
            P(("img", "pen"), None, None),
            P(("img", "pen"), None, None),
            P(("img", "pen")),
            P(("img", "pen"), None),
            P(("img", "pen")),
            P(),
            P(),
            P(),
        ),
        out_specs=P("pen", "img", None),
        check_vma=False,
    )
```

profile of v0, /device:TPU:1, one launch (start us, length us, event | category | flops | bytes accessed | tf_op | source)
XLA Modules:
  0.0 989.2 jit_solution(1041263062261779404)
XLA Ops:
  3.5 11.5 %all-to-all-start = ((s32[128,2,1]{1,2,0:T(1,128)}), s32[128,2,1]{1,2,0:T(1,128)S(1)}, u32[]{:S(2)}, u32[]{:S(2)}) async-start(s32[128,2,1]{1,2,0:T(1,128)} %bitcast.8), calls=%async_computation | async-start | bytes 131072 | tf_op jit(solution)/shard_map/all_to_all | solution.py:52
  24.4 11.6 %gather_fusion.1 = bf16[128,128,384]{2,1,0:T(8,128)(2,1)} fusion(bf16[64,128,384]{2,1,0:T(8,128)(2,1)} %pad_maximum_fusion, s32[1024]{0:T(1024)S(1)} %pad_clamp_fusion), kind=kCustom, calls=%fused_computation.1 | custom fusion | bytes 25166336 | tf_op jit(solution)/shard_map/gather | solution.py:36
  36.0 9.0 convolution_convert_fusion
  59.0 8.9 gather_fusion.2
  67.9 11.7 %fusion.2 = bf16[128,48,3,384]{3,1,2,0:T(8,128)(2,1)} fusion(bf16[128,48,3,128]{3,1,2,0:T(8,128)(2,1)} %copy.70, bf16[128,128,384]{2,1,0:T(8,128)(2,1)} %gather_fusion.2), kind=kOutput, calls=%fused_computation.8 | convolution fusion | flops 1819017216 | bytes 31457280 | tf_op jit(solution)/shard_map/sycp,spq->sycq/dot_general | solution.py:41
  79.6 19.4 %copy.71 = bf16[128,48,3,384]{0,3,2,1:T(8,128)(2,1)} copy(bf16[128,48,3,384]{3,1,2,0:T(8,128)(2,1)} %fusion.2) | data formatting | bytes 28311552 | tf_op jit(solution)/shard_map/convert_element_type | solution.py:44
  99.0 18.6 %copy.72 = bf16[128,48,1152]{2,1,0:T(8,128)(2,1)} copy(bf16[128,48,1152]{0,2,1:T(8,128)(2,1)} %bitcast.105) | data formatting | bytes 28311552 | tf_op jit(solution)/shard_map/reshape | solution.py:44
  117.6 9.3 broadcast_in_dim.17
  127.0 41.3 %scatter_fusion = bf16[256,48,1152]{2,1,0:T(8,128)(2,1)} fusion(bf16[256,48,1152]{2,1,0:T(8,128)(2,1)} %broadcast_in_dim.17, s32[128]{0:T(128)S(1)} %fusion.52, bf16[128,48,1152]{2,1,0:T(8,128)(2,1)} %copy.72), kind=kCustom, calls=%fused_computation.4 | custom fusion | bytes 42467840 | tf_op jit(solution)/shard_map/scatter | solution.py:47
  168.2 10.1 %all-to-all-start.1 = ((bf16[256,48,1152]{2,1,0:T(8,128)(2,1)}), bf16[256,48,1152]{2,1,0:T(8,128)(2,1)}, u32[]{:S(2)}, u32[]{:S(2)}) async-start(bf16[256,48,1152]{2,1,0:T(8,128)(2,1)} %scatter_fusion), calls=%async_computation.1 | async-start | bytes 56623104 | tf_op jit(solution)/shard_map/all_to_all | solution.py:51
  185.9 8.2 copy.77
  202.5 358.7 %all-to-all-done.1 = bf16[256,48,1152]{2,1,0:T(8,128)(2,1)} async-done(((bf16[256,48,1152]{2,1,0:T(8,128)(2,1)}), bf16[256,48,1152]{2,1,0:T(8,128)(2,1)}, u32[]{:S(2)}, u32[]{:S(2)}) %all-to-all-start.1) | async-done | bytes 28311584 | tf_op jit(solution)/shard_map/all_to_all | solution.py:51
  561.1 35.8 %copy.94 = bf16[256,48,1152]{0,2,1:T(8,128)(2,1)} copy(bf16[256,48,1152]{2,1,0:T(8,128)(2,1)} %all-to-all-done.1) | data formatting | bytes 56623104 | tf_op jit(solution)/shard_map/reshape | solution.py:59
  596.9 14.8 %fusion.36 = f32[16,48,3,384]{3,0,2,1:T(8,128)} fusion(bf16[48,3,384,256]{3,2,1,0:T(8,128)(2,1)} %bitcast.104, s32[256]{0:T(256)S(1)} %eq.56, bf16[16,128]{1,0:T(8,128)(2,1)S(1)} %copy-done.3, s32[]{:T(128)S(6)} %select_n.105), kind=kOutput, calls=%fused_computation.55 | convolution fusion | flops 453124096 | bytes 31855620 | tf_op jit(solution)/shard_map/dot_general | solution.py:58
  614.6 15.2 %fusion.9 = f32[16,48,1536]{2,0,1:T(8,128)} fusion(f32[768,1536]{0,1:T(8,128)} %reshape.300, f32[16,48,384]{2,0,1:T(8,128)S(1)} %fusion.27, f32[16,48,384]{2,0,1:T(8,128)S(1)} %fusion.30), kind=kOutput, calls=%fused_computation.18 | convolution fusion | flops 10872225792 | bytes 11796480 | tf_op jit(solution)/shard_map/dot_general | solution.py:81
  629.9 11.2 %copy.80 = f32[16,48,1536]{1,0,2:T(8,128)} copy(f32[16,48,1536]{2,0,1:T(8,128)} %fusion.9) | data formatting | bytes 9437184 | tf_op jit(solution)/shard_map/dot_general | solution.py:81
  641.0 17.6 %reshape.364 = f32[16,1,73728]{2,1,0:T(1,128)} reshape(f32[1536,16,48]{2,1,0:T(8,128)} %bitcast.109) | data formatting | bytes 9437184
  658.7 19.8 %all-to-all-start.2 = ((f32[16,1,73728]{2,1,0:T(1,128)}), f32[16,1,73728]{2,1,0:T(1,128)}, u32[]{:S(2)}, u32[]{:S(2)}) async-start(f32[16,1,73728]{2,1,0:T(1,128)} %reshape.364), calls=%async_computation.2 | async-start | bytes 9437184 | tf_op jit(solution)/shard_map/all_to_all | solution.py:84
  678.5 9.0 fusion.35
  687.4 9.7 fusion.19
  701.6 46.3 %all-to-all-done.2 = f32[16,1,73728]{2,1,0:T(1,128)} async-done(((f32[16,1,73728]{2,1,0:T(1,128)}), f32[16,1,73728]{2,1,0:T(1,128)}, u32[]{:S(2)}, u32[]{:S(2)}) %all-to-all-start.2) | async-done | bytes 4718624 | tf_op jit(solution)/shard_map/all_to_all | solution.py:84
  748.4 15.8 %reduce.4 = f32[16,73728]{1,0:T(8,128)} reduce(f32[16,1,73728]{2,1,0:T(1,128)} %all-to-all-done.2, f32[]{:T(128)} %broadcast.367), dimensions={1}, to_apply=%all_to_all.36.reduce_sub_computation | reduce | bytes 9437188 | tf_op jit(solution)/shard_map/all_to_all | solution.py:84
  764.2 14.1 %reshape.365 = f32[1536,16,48]{2,1,0:T(8,128)} reshape(f32[16,73728]{1,0:T(8,128)} %reduce.4) | data formatting | bytes 9437184
  778.3 16.3 %copy.106 = f32[16,48,16,96]{1,2,0,3:T(8,128)} copy(f32[16,48,16,96]{1,0,3,2:T(8,128)} %bitcast.106) | data formatting | bytes 9437184 | tf_op jit(solution)/shard_map/all_to_all | solution.py:84
  794.6 10.9 %reshape.301 = f32[16,768,48,2]{1,0,3,2:T(8,128)} reshape(f32[16,16,48,96]{2,1,0,3:T(8,128)} %bitcast.107) | data formatting | bytes 9437184 | tf_op jit(solution)/shard_map/reshape | solution.py:86
  805.5 42.1 %fusion.22 = f32[16,768,48,2]{1,2,0,3:T(8,128)} fusion(f32[16,768,48,2]{1,0,3,2:T(8,128)} %reshape.301, f32[768,1,768,2]{2,0,1,3:T(8,128)} %get-tuple-element.6, f32[768,1,768,2]{2,0,1,3:T(8,128)} %get-tuple-element.5), kind=kOutput, calls=%fused_computation.35 | convolution fusion | flops 21745631232 | bytes 18874368 | tf_op jit(solution)/shard_map/nkxc,kcyd->nyxd/dot_general | solution.py:87
  847.7 12.0 %copy.83 = f32[16,768,48,2]{2,0,3,1:T(8,128)} copy(f32[16,768,48,2]{1,2,0,3:T(8,128)} %fusion.22) | data formatting | bytes 9437184 | tf_op jit(solution)/shard_map/nkxc,kcyd->nyxd/transpose | solution.py:87
  859.7 14.4 %reshape.366 = f32[8,1,147456]{2,1,0:T(1,128)} reshape(f32[768,2,16,48]{3,2,1,0:T(8,128)} %bitcast.110) | data formatting | bytes 9437184
  880.9 54.1 %all-to-all-done.3 = f32[8,1,147456]{2,1,0:T(1,128)} async-done(((f32[8,1,147456]{2,1,0:T(1,128)}), f32[8,1,147456]{2,1,0:T(1,128)}, u32[]{:S(2)}, u32[]{:S(2)}) %all-to-all-start.3) | async-done | bytes 4718624 | tf_op jit(solution)/shard_map/all_to_all | solution.py:92
  935.0 15.7 %reduce.5 = f32[8,147456]{1,0:T(8,128)} reduce(f32[8,1,147456]{2,1,0:T(1,128)} %all-to-all-done.3, f32[]{:T(128)} %broadcast.367), dimensions={1}, to_apply=%all_to_all.39.reduce_sub_computation | reduce | bytes 9437188 | tf_op jit(solution)/shard_map/all_to_all | solution.py:92
  950.7 11.9 %reshape.367 = f32[768,2,16,48]{3,2,1,0:T(8,128)} reshape(f32[8,147456]{1,0:T(8,128)} %reduce.5) | data formatting | bytes 9437184
  962.6 11.9 %copy.84 = f32[16,8,96,48,2]{2,3,4,0,1:T(8,128)} copy(f32[16,8,96,48,2]{3,0,4,2,1:T(8,128)} %bitcast.108) | data formatting | bytes 9437184 | tf_op jit(solution)/shard_map/all_to_all | solution.py:92
  (36 shorter events, 71.6 us)
Async XLA Ops:
  0.0 59.0 %copy-start = (bf16[16,128,384]{2,1,0:T(8,128)(2,1)S(1)}, bf16[16,128,384]{2,1,0:T(8,128)(2,1)}, u32[]{:S(2)}) copy-start(bf16[16,128,384]{2,1,0:T(8,128)(2,1)} %param.14) | copy-start | bytes 4718596
  3.5 164.7 %all-to-all-start = ((s32[128,2,1]{1,2,0:T(1,128)}), s32[128,2,1]{1,2,0:T(1,128)S(1)}, u32[]{:S(2)}, u32[]{:S(2)}) async-start(s32[128,2,1]{1,2,0:T(1,128)} %bitcast.8), calls=%async_computation | async-start | bytes 131072 | tf_op jit(solution)/shard_map/all_to_all | solution.py:52
  168.2 392.9 %all-to-all-start.1 = ((bf16[256,48,1152]{2,1,0:T(8,128)(2,1)}), bf16[256,48,1152]{2,1,0:T(8,128)(2,1)}, u32[]{:S(2)}, u32[]{:S(2)}) async-start(bf16[256,48,1152]{2,1,0:T(8,128)(2,1)} %scatter_fusion), calls=%async_computation.1 | async-start | bytes 56623104 | tf_op jit(solution)/shard_map/all_to_all | solution.py:51
  202.4 394.5 %copy-start.3 = (bf16[16,128]{1,0:T(8,128)(2,1)S(1)}, bf16[16,128]{1,0:T(8,128)(2,1)}, u32[]{:S(2)}) copy-start(bf16[16,128]{1,0:T(8,128)(2,1)} %param.15) | copy-start | bytes 12292
  611.8 2.7 copy-start.2
  658.7 89.2 %all-to-all-start.2 = ((f32[16,1,73728]{2,1,0:T(1,128)}), f32[16,1,73728]{2,1,0:T(1,128)}, u32[]{:S(2)}, u32[]{:S(2)}) async-start(f32[16,1,73728]{2,1,0:T(1,128)} %reshape.364), calls=%async_computation.2 | async-start | bytes 9437184 | tf_op jit(solution)/shard_map/all_to_all | solution.py:84
  874.1 61.0 %all-to-all-start.3 = ((f32[8,1,147456]{2,1,0:T(1,128)}), f32[8,1,147456]{2,1,0:T(1,128)}, u32[]{:S(2)}, u32[]{:S(2)}) async-start(f32[8,1,147456]{2,1,0:T(1,128)} %reshape.366), calls=%async_computation.3 | async-start | bytes 9437184 | tf_op jit(solution)/shard_map/all_to_all | solution.py:92
  974.5 14.2 %copy-start.1 = (bf16[16,128,384]{2,1,0:T(8,128)(2,1)S(1)}, bf16[16,128,384]{2,1,0:T(8,128)(2,1)}, u32[]{:S(2)}) copy-start(bf16[16,128,384]{2,1,0:T(8,128)(2,1)} %param.14) | copy-start | bytes 4718596
where the time goes:
time: 1000 us; the launch traced here: 989 us
  waiting for transfers between devices  459 us (46%)
  local copies, waits for them, and re-layouts  307 us (31%)
  matrix products  100 us (10%)
  other arithmetic  74.4 us (7%)
  starting transfers between devices  47.9 us (5%)
    all_to_all x1, waiting for transfers between devices, local(): lax.all_to_all(outgoing, ('img', 'pen'), split_axis=0, concat_axis=0, til...  359 us
    unnamed x12, local copies, waits for them, and re-layouts  58.9 us
    all_to_all x1, waiting for transfers between devices, local(): lax.all_to_all(after_y.reshape(planes, NBOX, -1, 2), 'pen', split_axis=1,...  54.1 us
    all_to_all x1, waiting for transfers between devices, local(): lax.all_to_all(after_x, 'img', split_axis=2, concat_axis=1, tiled=True)  46.3 us
    dot_general x1, matrix products, local(): jnp.einsum('nkxc,kcyd->nyxd', shaped, table_y, precision=lax.Precision.HI...  42.1 us
    scatter x1, local copies, waits for them, and re-layouts, local(): jnp.zeros((slot_total, rows_brick, tile_width), jnp.bfloat16).at[slot_index]  41.3 us
    reshape x1, local copies, waits for them, and re-layouts, local(): incoming.reshape(slot_total, -1)  35.8 us
  transfers between devices with their start and end apart: 4, of which 3 were waited for; matrix products, arithmetic and copies ran while one was open for 20% of the time, Pallas kernels for 0%

commit v1 on v0

--- a/solution.py
+++ b/solution.py
@@ -27,36 +27,38 @@
     window = z_bank.shape[1]
     planes = window // pen_count
     slot_total = bricks * CAP
-    images = jnp.concatenate([slice_tiles, ctf_tiles], axis=2)
     target = entry_brick[:, 0]
     positions = jnp.arange(entry_count, dtype=jnp.int32)
     earlier = (target[None, :] == target[:, None]) & (positions[None, :] < positions[:, None])
     slot_rank = jnp.sum(earlier.astype(jnp.int32), axis=1)
     slot_index = target * CAP + slot_rank
-    pixels = images[entry_tile]
-    half_tile = jnp.einsum(
-        "eyp,epc->eyc", ky_bank[entry_kernel], pixels, preferred_element_type=jnp.float32
+    owner = jnp.full((slot_total,), entry_count, jnp.int32).at[slot_index].set(positions)
+    filled = owner < entry_count
+    source = jnp.minimum(owner, entry_count - 1)
+    tile_of = entry_tile[source]
+    kernel_of = jnp.where(filled, entry_kernel[source], 0)
+    rows_ky = ky_bank[kernel_of] * filled[:, None, None].astype(ky_bank.dtype)
+    half_slice = jnp.einsum(
+        "syp,spc->syc", rows_ky, slice_tiles[tile_of], preferred_element_type=jnp.float32
     ).astype(jnp.bfloat16)
-    shaped = half_tile.reshape(half_tile.shape[0], rows_brick, 3, PIX)
-    gridded = jnp.einsum(
-        "sycp,spq->sycq", shaped, kx_bank[entry_kernel], preferred_element_type=jnp.float32
-    )
-    payload = gridded.astype(jnp.bfloat16).reshape(half_tile.shape[0], rows_brick, 3 * KXH)
-    tile_width = payload.shape[2]
-    outgoing = (
-        jnp.zeros((slot_total, rows_brick, tile_width), jnp.bfloat16).at[slot_index].set(payload)
-    )
-    labels = jnp.zeros((slot_total,), jnp.int32).at[slot_index].set(entry_kernel)
+    half_ctf = jnp.einsum(
+        "syp,spc->syc", rows_ky, ctf_tiles[tile_of], preferred_element_type=jnp.float32
+    ).astype(jnp.bfloat16)
+    outgoing = jnp.concatenate([half_slice, half_ctf], axis=2)
     incoming, kind_ids = (
         lax.all_to_all(outgoing, ("img", "pen"), split_axis=0, concat_axis=0, tiled=True),
-        lax.all_to_all(labels, ("img", "pen"), split_axis=0, concat_axis=0, tiled=True),
+        lax.all_to_all(kernel_of, ("img", "pen"), split_axis=0, concat_axis=0, tiled=True),
     )
+    shaped = incoming.reshape(slot_total, rows_brick, 3, PIX)
+    gridded = jnp.einsum(
+        "sycp,spq->sycq", shaped, kx_bank[kind_ids], preferred_element_type=jnp.float32
+    ).astype(jnp.bfloat16)
     plane_start = lax.axis_index("pen") * planes
     z_columns = lax.dynamic_slice_in_dim(z_bank, plane_start, planes, 1)
     onehot = (kind_ids[:, None] == jnp.arange(NK, dtype=jnp.int32)[None, :]).astype(jnp.bfloat16)
     weights_z = jnp.dot(onehot, z_columns, preferred_element_type=jnp.float32).astype(jnp.bfloat16)
     brick_sums = jnp.dot(
-        weights_z.T, incoming.reshape(slot_total, -1), preferred_element_type=jnp.float32
+        weights_z.T, gridded.reshape(slot_total, -1), preferred_element_type=jnp.float32
     ).reshape(planes, rows_brick, 3, KXH)
     denominator = brick_sums[:, :, 2] + 1.0
     grid_real = brick_sums[:, :, 0] / denominator

time: 1000 us -> 682 us (0.68)
  waiting for transfers between devices: 459 us -> 177 us
  local copies, waits for them, and re-layouts: 307 us -> 245 us
  matrix products: 100 us -> 135 us
  starting transfers between devices: 47.9 us -> 35.3 us
    all_to_all x1, waiting for transfers between devices: 359 us -> 73 us  [local(): lax.all_to_all(outgoing, ('img', 'pen'), split_axis=0, concat_axis=0, til...]
    reshape x3 -> x1, local copies, waits for them, and re-layouts: 61.5 us -> 12.7 us  [local(): shaped = incoming.reshape(slot_total, rows_brick, 3, PIX)]
    scatter x2 -> x1, local copies, waits for them, and re-layouts: 42.4 us -> 0.97 us  [local(): jnp.full((slot_total,), entry_count, jnp.int32).at[slot_index]]
    dot_general x3 -> x4, matrix products: 35.5 us -> 70.1 us  [the longest x1 35.9 us: local(): jnp.einsum('sycp,spq->sycq', shaped, kx_bank[kind_ids], preferred_element...]
    gather x3 -> x6, local copies, waits for them, and re-layouts: 22.3 us -> 38.9 us  [the longest x1 12.4 us: local(): kx_bank[kind_ids]]
    all_to_all x2 -> x4, local copies, waits for them, and re-layouts: 1.28 us -> 14.3 us  [the longest x1 12.9 us: local(): lax.all_to_all(outgoing, ('img', 'pen'), split_axis=0, concat_axis=0, til...]
    all_to_all x1, starting transfers between devices: 19.8 us -> 8.14 us  [local(): lax.all_to_all(after_x, 'img', split_axis=2, concat_axis=1, tiled=True)]
    convert_element_type x2 -> x1, local copies, waits for them, and re-layouts: 26.4 us -> 35.3 us  [local(): gridded = jnp.einsum('sycp,spq->sycq', shaped, kx_bank[kind_ids], preferr...]
  transfers between devices with their start and end apart: 4 -> 4, of which waited for: 3 -> 3; matrix products, arithmetic and copies ran while one was open for 20% -> 17% of each run, Pallas kernels for 0% -> 0%
where the time goes in v1:
time: 682 us; the launch traced here: 669 us
  local copies, waits for them, and re-layouts  245 us (36%)
  waiting for transfers between devices  177 us (26%)
  matrix products  135 us (20%)
  other arithmetic  75.5 us (11%)
  starting transfers between devices  35.3 us (5%)
    all_to_all x1, waiting for transfers between devices, local(): lax.all_to_all(outgoing, ('img', 'pen'), split_axis=0, concat_axis=0, til...  73 us
    unnamed x18, local copies, waits for them, and re-layouts  58.6 us
    all_to_all x1, waiting for transfers between devices, local(): lax.all_to_all(after_y.reshape(planes, NBOX, -1, 2), 'pen', split_axis=1,...  54.1 us
    all_to_all x1, waiting for transfers between devices, local(): lax.all_to_all(after_x, 'img', split_axis=2, concat_axis=1, tiled=True)  49.8 us
    dot_general x1, matrix products, local(): jnp.einsum('nkxc,kcyd->nyxd', shaped, table_y, precision=lax.Precision.HI...  42.2 us
    dot_general x1, matrix products, local(): jnp.einsum('sycp,spq->sycq', shaped, kx_bank[kind_ids], preferred_element...  35.9 us
    convert_element_type x1, local copies, waits for them, and re-layouts, local(): gridded = jnp.einsum('sycp,spq->sycq', shaped, kx_bank[kind_ids], preferr...  35.3 us
    all_to_all x2, local copies, waits for them, and re-layouts, local(): lax.all_to_all(after_y.reshape(planes, NBOX, -1, 2), 'pen', split_axis=1,...  18.4 us
  transfers between devices with their start and end apart: 4, of which 3 were waited for; matrix products, arithmetic and copies ran while one was open for 17% of the time, Pallas kernels for 0%

profile of v1, /device:TPU:1, one launch (start us, length us, event | category | flops | bytes accessed | tf_op | source)
XLA Modules:
  0.0 668.7 jit_solution(14327910729315700961)
XLA Ops:
  5.4 11.5 %all-to-all-start = ((s32[128,2,1]{1,2,0:T(1,128)}), s32[128,2,1]{1,2,0:T(1,128)S(1)}, u32[]{:S(2)}, u32[]{:S(2)}) async-start(s32[128,2,1]{1,2,0:T(1,128)} %bitcast.8), calls=%async_computation | async-start | bytes 131072 | tf_op jit(solution)/shard_map/all_to_all | solution.py:50
  18.8 11.6 %gather_fusion.3 = bf16[256,128,256]{2,1,0:T(8,128)(2,1)} fusion(bf16[64,128,256]{2,1,0:T(8,128)(2,1)} %param.8, s32[1024]{0:T(1024)S(1)} %pad_clamp_fusion.1), kind=kCustom, calls=%fused_computation.3 | custom fusion | bytes 33555456 | tf_op jit(solution)/shard_map/gather | solution.py:42
  30.4 8.4 %gather_fusion.4 = bf16[256,128,128]{2,1,0:T(8,128)(2,1)} fusion(bf16[64,128,128]{2,1,0:T(8,128)(2,1)S(1)} %copy-done, s32[1024]{0:T(1024)S(1)} %pad_clamp_fusion.1), kind=kCustom, calls=%fused_computation.4 | custom fusion | bytes 16778240 | tf_op jit(solution)/shard_map/gather | solution.py:45
  41.5 11.9 %convolution_convert_fusion = bf16[256,48,256]{2,1,0:T(8,128)(2,1)} fusion(bf16[256,128,256]{2,1,0:T(8,128)(2,1)} %gather_fusion.3, bf16[256,48,128]{2,1,0:T(8,128)(2,1)} %gather_fusion.1, bf16[256]{0:T(256)(128)(2,1)S(1)} %fusion.66), kind=kOutput, calls=%fused_computation.26 | convolution fusion | flops 810024960 | bytes 26214912 | tf_op jit(solution)/shard_map/syp,spc->syc/dot_general | solution.py:41
  60.9 8.3 %pad_maximum_fusion = bf16[256,48,384]{2,1,0:T(8,128)(2,1)} fusion(bf16[256,48,128]{2,1,0:T(8,128)(2,1)} %fusion.30, bf16[256,48,256]{2,1,0:T(8,128)(2,1)} %convolution_convert_fusion), kind=kLoop, calls=%fused_computation.17 | loop fusion | flops 18874368 | bytes 18874368 | tf_op jit(solution)/shard_map/concatenate | solution.py:47
  69.2 10.6 %all-to-all-start.1 = ((bf16[256,48,384]{2,1,0:T(8,128)(2,1)}), bf16[256,48,384]{2,1,0:T(8,128)(2,1)}, u32[]{:S(2)}, u32[]{:S(2)}) async-start(bf16[256,48,384]{2,1,0:T(8,128)(2,1)} %pad_maximum_fusion), calls=%async_computation.1 | async-start | bytes 18874368 | tf_op jit(solution)/shard_map/all_to_all | solution.py:49
  87.4 8.2 %copy.69 = f32[768,768,2]{0,2,1:T(2,128)} copy(f32[768,768,2]{1,0,2:T(8,128)} %maximum_maximum_fusion) | data formatting | bytes 9437184 | tf_op jit(solution)/shard_map/concatenate | solution.py:72
  104.2 12.4 %gather_fusion.5 = bf16[256,128,384]{2,1,0:T(8,128)(2,1)} fusion(bf16[16,128,384]{2,1,0:T(8,128)(2,1)S(1)} %copy-done.2, s32[1024]{0:T(1024)S(1)} %pad_clamp_fusion), kind=kCustom, calls=%fused_computation.5 | custom fusion | bytes 50332672 | tf_op jit(solution)/shard_map/gather | solution.py:54
  116.7 73.0 %all-to-all-done.1 = bf16[256,48,384]{2,1,0:T(8,128)(2,1)} async-done(((bf16[256,48,384]{2,1,0:T(8,128)(2,1)}), bf16[256,48,384]{2,1,0:T(8,128)(2,1)}, u32[]{:S(2)}, u32[]{:S(2)}) %all-to-all-start.1) | async-done | bytes 9437216 | tf_op jit(solution)/shard_map/all_to_all | solution.py:49
  189.6 12.9 %copy.63 = bf16[256,48,384]{0,2,1:T(8,128)(2,1)} copy(bf16[256,48,384]{2,1,0:T(8,128)(2,1)} %all-to-all-done.1) | data formatting | bytes 18874368 | tf_op jit(solution)/shard_map/all_to_all | solution.py:49
  202.5 12.7 %copy.64 = bf16[256,48,3,128]{3,1,2,0:T(8,128)(2,1)} copy(bf16[256,48,3,128]{0,3,2,1:T(8,128)(2,1)} %bitcast.113) | data formatting | bytes 18874368 | tf_op jit(solution)/shard_map/reshape | solution.py:52
  215.2 35.9 %fusion.4 = bf16[256,48,3,384]{3,1,2,0:T(8,128)(2,1)} fusion(bf16[256,48,3,128]{3,1,2,0:T(8,128)(2,1)} %copy.64, bf16[256,128,384]{2,1,0:T(8,128)(2,1)} %gather_fusion.5), kind=kOutput, calls=%fused_computation.11 | convolution fusion | flops 3638034432 | bytes 62914560 | tf_op jit(solution)/shard_map/sycp,spq->sycq/dot_general | solution.py:53
  251.1 35.3 %copy.65 = bf16[256,48,3,384]{0,3,2,1:T(8,128)(2,1)} copy(bf16[256,48,3,384]{3,1,2,0:T(8,128)(2,1)} %fusion.4) | data formatting | bytes 56623104 | tf_op jit(solution)/shard_map/convert_element_type | solution.py:55
  286.4 14.9 %fusion = f32[16,48,3,384]{3,0,2,1:T(8,128)} fusion(bf16[256,48,3,384]{0,3,2,1:T(8,128)(2,1)} %copy.65, s32[256]{0:T(256)S(1)} %eq.56, bf16[16,128]{1,0:T(8,128)(2,1)S(1)} %copy-done.6, s32[]{:T(128)S(6)} %select_n.131), kind=kOutput, calls=%fused_computation.7 | convolution fusion | flops 453124096 | bytes 31855620 | tf_op jit(solution)/shard_map/dot_general | solution.py:60
  304.1 14.8 %fusion.11 = f32[16,48,1536]{2,0,1:T(8,128)} fusion(f32[768,1536]{0,1:T(8,128)} %reshape.339, f32[16,48,384]{2,0,1:T(8,128)S(1)} %fusion.37, f32[16,48,384]{2,0,1:T(8,128)S(1)} %fusion.40), kind=kOutput, calls=%fused_computation.22 | convolution fusion | flops 10872225792 | bytes 11796480 | tf_op jit(solution)/shard_map/dot_general | solution.py:83
  319.0 11.2 %copy.72 = f32[16,48,1536]{1,0,2:T(8,128)} copy(f32[16,48,1536]{2,0,1:T(8,128)} %fusion.11) | data formatting | bytes 9437184 | tf_op jit(solution)/shard_map/dot_general | solution.py:83
  330.2 17.6 %reshape.422 = f32[16,1,73728]{2,1,0:T(1,128)} reshape(f32[1536,16,48]{2,1,0:T(8,128)} %bitcast.111) | data formatting | bytes 9437184
  347.8 8.1 %all-to-all-start.2 = ((f32[16,1,73728]{2,1,0:T(1,128)}), f32[16,1,73728]{2,1,0:T(1,128)}, u32[]{:S(2)}, u32[]{:S(2)}) async-start(f32[16,1,73728]{2,1,0:T(1,128)} %reshape.422), calls=%async_computation.2 | async-start | bytes 9437184 | tf_op jit(solution)/shard_map/all_to_all | solution.py:86
  356.0 9.0 %fusion.45 = f32[768,768,1]{1,0,2:T(8,128)S(1)} fusion(), kind=kLoop, calls=%fused_computation.64 | loop fusion | flops 5898240 | bytes 2359296 | tf_op jit(solution)/shard_map/neg | solution.py:78
  364.9 9.9 %fusion.24 = (f32[768,768,1]{1,0,2:T(8,128)S(1)}, f32[768,768,1]{1,0,2:T(8,128)S(1)}) fusion(), kind=kLoop, calls=%fused_computation.39 | loop fusion | flops 5308416 | bytes 4718592 | tf_op jit(solution)/shard_map/sin | solution.py:77
  379.2 49.8 %all-to-all-done.2 = f32[16,1,73728]{2,1,0:T(1,128)} async-done(((f32[16,1,73728]{2,1,0:T(1,128)}), f32[16,1,73728]{2,1,0:T(1,128)}, u32[]{:S(2)}, u32[]{:S(2)}) %all-to-all-start.2) | async-done | bytes 4718624 | tf_op jit(solution)/shard_map/all_to_all | solution.py:86
  429.5 15.8 %reduce.6 = f32[16,73728]{1,0:T(8,128)} reduce(f32[16,1,73728]{2,1,0:T(1,128)} %all-to-all-done.2, f32[]{:T(128)} %broadcast.428), dimensions={1}, to_apply=%all_to_all.39.reduce_sub_computation | reduce | bytes 9437188 | tf_op jit(solution)/shard_map/all_to_all | solution.py:86
  445.2 13.9 %reshape.423 = f32[1536,16,48]{2,1,0:T(8,128)} reshape(f32[16,73728]{1,0:T(8,128)} %reduce.6) | data formatting | bytes 9437184
  459.1 16.3 %copy.97 = f32[16,48,16,96]{1,2,0,3:T(8,128)} copy(f32[16,48,16,96]{1,0,3,2:T(8,128)} %bitcast.108) | data formatting | bytes 9437184 | tf_op jit(solution)/shard_map/all_to_all | solution.py:86
  475.4 10.9 %reshape.340 = f32[16,768,48,2]{1,0,3,2:T(8,128)} reshape(f32[16,16,48,96]{2,1,0,3:T(8,128)} %bitcast.109) | data formatting | bytes 9437184 | tf_op jit(solution)/shard_map/reshape | solution.py:88
  486.4 42.2 %fusion.27 = f32[16,768,48,2]{1,2,0,3:T(8,128)} fusion(f32[16,768,48,2]{1,0,3,2:T(8,128)} %reshape.340, f32[768,1,768,2]{2,0,1,3:T(8,128)} %get-tuple-element.8, f32[768,1,768,2]{2,0,1,3:T(8,128)} %get-tuple-element.7), kind=kOutput, calls=%fused_computation.42 | convolution fusion | flops 21745631232 | bytes 18874368 | tf_op jit(solution)/shard_map/nkxc,kcyd->nyxd/dot_general | solution.py:89
  528.5 12.0 %copy.75 = f32[16,768,48,2]{2,0,3,1:T(8,128)} copy(f32[16,768,48,2]{1,2,0,3:T(8,128)} %fusion.27) | data formatting | bytes 9437184 | tf_op jit(solution)/shard_map/nkxc,kcyd->nyxd/transpose | solution.py:89
  540.6 14.4 %reshape.424 = f32[8,1,147456]{2,1,0:T(1,128)} reshape(f32[768,2,16,48]{3,2,1,0:T(8,128)} %bitcast.112) | data formatting | bytes 9437184
  560.4 54.1 %all-to-all-done.3 = f32[8,1,147456]{2,1,0:T(1,128)} async-done(((f32[8,1,147456]{2,1,0:T(1,128)}), f32[8,1,147456]{2,1,0:T(1,128)}, u32[]{:S(2)}, u32[]{:S(2)}) %all-to-all-start.3) | async-done | bytes 4718624 | tf_op jit(solution)/shard_map/all_to_all | solution.py:94
  614.5 15.7 %reduce.7 = f32[8,147456]{1,0:T(8,128)} reduce(f32[8,1,147456]{2,1,0:T(1,128)} %all-to-all-done.3, f32[]{:T(128)} %broadcast.428), dimensions={1}, to_apply=%all_to_all.42.reduce_sub_computation | reduce | bytes 9437188 | tf_op jit(solution)/shard_map/all_to_all | solution.py:94
  630.2 11.9 %reshape.425 = f32[768,2,16,48]{3,2,1,0:T(8,128)} reshape(f32[8,147456]{1,0:T(8,128)} %reduce.7) | data formatting | bytes 9437184
  642.1 11.9 %copy.76 = f32[16,8,96,48,2]{2,3,4,0,1:T(8,128)} copy(f32[16,8,96,48,2]{3,0,4,2,1:T(8,128)} %bitcast.110) | data formatting | bytes 9437184 | tf_op jit(solution)/shard_map/all_to_all | solution.py:94
  (49 shorter events, 60.9 us)
Async XLA Ops:
  0.0 30.4 %copy-start = (bf16[64,128,128]{2,1,0:T(8,128)(2,1)S(1)}, bf16[64,128,128]{2,1,0:T(8,128)(2,1)}, u32[]{:S(2)}) copy-start(bf16[64,128,128]{2,1,0:T(8,128)(2,1)} %param.9) | copy-start | bytes 6291460
  5.4 63.8 %all-to-all-start = ((s32[128,2,1]{1,2,0:T(1,128)}), s32[128,2,1]{1,2,0:T(1,128)S(1)}, u32[]{:S(2)}, u32[]{:S(2)}) async-start(s32[128,2,1]{1,2,0:T(1,128)} %bitcast.8), calls=%async_computation | async-start | bytes 131072 | tf_op jit(solution)/shard_map/all_to_all | solution.py:50
  30.4 8.5 %copy-start.3 = (bf16[16,48,128]{2,1,0:T(8,128)(2,1)S(1)}, bf16[16,48,128]{2,1,0:T(8,128)(2,1)}, u32[]{:S(2)}) copy-start(bf16[16,48,128]{2,1,0:T(8,128)(2,1)} %param.13) | copy-start | bytes 589828
  41.5 12.0 %copy-start.4 = (bf16[256,48,128]{2,1,0:T(8,128)(2,1)S(1)}, bf16[256,48,128]{2,1,0:T(8,128)(2,1)}, u32[]{:S(2)}) copy-start(bf16[256,48,128]{2,1,0:T(8,128)(2,1)} %gather_fusion.1) | copy-start | bytes 9437188
  69.2 120.5 %all-to-all-start.1 = ((bf16[256,48,384]{2,1,0:T(8,128)(2,1)}), bf16[256,48,384]{2,1,0:T(8,128)(2,1)}, u32[]{:S(2)}, u32[]{:S(2)}) async-start(bf16[256,48,384]{2,1,0:T(8,128)(2,1)} %pad_maximum_fusion), calls=%async_computation.1 | async-start | bytes 18874368 | tf_op jit(solution)/shard_map/all_to_all | solution.py:49
  95.6 8.6 %copy-start.2 = (bf16[16,128,384]{2,1,0:T(8,128)(2,1)S(1)}, bf16[16,128,384]{2,1,0:T(8,128)(2,1)}, u32[]{:S(2)}) copy-start(bf16[16,128,384]{2,1,0:T(8,128)(2,1)} %param.14) | copy-start | bytes 4718596
  251.1 35.3 %copy-start.6 = (bf16[16,128]{1,0:T(8,128)(2,1)S(1)}, bf16[16,128]{1,0:T(8,128)(2,1)}, u32[]{:S(2)}) copy-start(bf16[16,128]{1,0:T(8,128)(2,1)} %param.15) | copy-start | bytes 12292
  301.2 2.7 copy-start.5
  347.8 81.2 %all-to-all-start.2 = ((f32[16,1,73728]{2,1,0:T(1,128)}), f32[16,1,73728]{2,1,0:T(1,128)}, u32[]{:S(2)}, u32[]{:S(2)}) async-start(f32[16,1,73728]{2,1,0:T(1,128)} %reshape.422), calls=%async_computation.2 | async-start | bytes 9437184 | tf_op jit(solution)/shard_map/all_to_all | solution.py:86
  555.0 59.5 %all-to-all-start.3 = ((f32[8,1,147456]{2,1,0:T(1,128)}), f32[8,1,147456]{2,1,0:T(1,128)}, u32[]{:S(2)}, u32[]{:S(2)}) async-start(f32[8,1,147456]{2,1,0:T(1,128)} %reshape.424), calls=%async_computation.3 | async-start | bytes 9437184 | tf_op jit(solution)/shard_map/all_to_all | solution.py:94
  660.5 7.7 %copy-start.1 = (bf16[64,128,128]{2,1,0:T(8,128)(2,1)S(1)}, bf16[64,128,128]{2,1,0:T(8,128)(2,1)}, u32[]{:S(2)}) copy-start(bf16[64,128,128]{2,1,0:T(8,128)(2,1)} %param.9) | copy-start | bytes 6291460
